TPU v7x, 32 devices: a whole 2x2x4 slice. The times are simulated.
32 devices in a mesh: node: 8 (over z, x), feat: 4 (over y, core).
Axes of the slice: x: 2, y: 2, z: 4, core: 2. Of those that a mesh axis runs over, the one named last changes fastest.
Arguments:
- feature_table: bfloat16 [8192, 2048], P('node', 'feat'), may hold values from -6 to 6
- hub_table: bfloat16 [32, 2048], P('node', 'feat'), may hold values from -6 to 6
- first_self: bfloat16 [2048, 2048], P('feat'), may hold values from -0.125 to 0.125
- first_pooled: bfloat16 [2048, 2048], P('feat'), may hold values from -0.125 to 0.125
- second_self: bfloat16 [2048, 256], P('feat'), may hold values from -0.125 to 0.125
- second_pooled: bfloat16 [2048, 256], P('feat'), may hold values from -0.125 to 0.125
- first_lists: int32 [3072, 10], P('node'), may hold values from 0 to 8223, as said below
- first_counts: int32 [3072], P('node'), may hold values from 1 to 10
- second_lists: int32 [2048, 5], P('node'), may hold values from 0 to 3071, as said below
- second_counts: int32 [2048], P('node'), may hold values from 1 to 5
Outputs:
- embedding: bfloat16 [2048, 256], P(('node', 'feat'))
Inputs may be any that keep to these rules, and one draw needn't show every extreme that they name: `first_lists`: an entry below 8192 names a row of feature_table, held by node shard (entry // 1024); an entry v of 8192 or more names hub clip v - 8192, owned by node shard (v - 8192) // 4. Slots at or beyond a clip's count are padding and still hold such entries. Of the 3840 entries of one node shard's rows, padding included, at most 480 name feature rows held by any one node shard; in every draw one node shard is named exactly 480 times by the rows of every node shard. `second_lists`: entries name frontier clips, held by node shard (entry // 384). Of the 1280 entries of one node shard's rows, padding included, exactly 160 name frontier clips of each node shard.
All inputs are finite; a program needn't handle non-finite values.
Results may differ from a plain program's by a relative error of at most 0.0052.
Values may be sent and summed in bfloat16 or wider, within the bound.
A program may use at most 64 MiB of HBM per device.

v0:
```python
import jax
import jax.numpy as jnp
from jax import lax
from jax.sharding import PartitionSpec as P


def count_matrix(local, width):
    columns = jnp.arange(width, dtype=jnp.int32)[None, :]
    total = jnp.zeros((local.shape[0], width), jnp.float32)
    for k in range(local.shape[1]):
        total = total + (local[:, k : k + 1] == columns).astype(jnp.float32)
    return total.astype(jnp.bfloat16)


def body(
    feature_table,
    hub_table,
    first_self,
    first_pooled,
    second_self,
    second_pooled,
    first_lists,
    first_counts,
    second_lists,
    second_counts,
):
    shards = lax.axis_size("node")
    me = lax.axis_index("node")
    rows_here = feature_table.shape[0]
    hubs_here = hub_table.shape[0]
    front_here, fan_one = first_lists.shape
    targets_here, fan_two = second_lists.shape
    total_rows = rows_here * shards
    slots_one = jnp.arange(fan_one, dtype=jnp.int32)[None, :]
    slots_two = jnp.arange(fan_two, dtype=jnp.int32)[None, :]
    lists_one = jnp.where(slots_one < first_counts[:, None], first_lists, -1)
    lists_two = jnp.where(slots_two < second_counts[:, None], second_lists, -1)
    packed = jnp.concatenate([lists_one.reshape(-1), lists_two.reshape(-1), second_counts]).reshape(
        1, -1
    )
    everyone = lax.all_gather(packed, "node", axis=0, tiled=True)
    cut_one = front_here * fan_one
    cut_two = cut_one + targets_here * fan_two
    all_one = everyone[:, :cut_one].reshape(shards * front_here, fan_one)
    all_two = everyone[:, cut_one:cut_two].reshape(shards * targets_here, fan_two)
    all_counts = everyone[:, cut_two:].reshape(shards * targets_here, 1)
    feature_at = all_one - me * rows_here
    hub_at = all_one - total_rows - me * hubs_here
    local_one = jnp.where(
        (feature_at >= 0) & (feature_at < rows_here) & (all_one >= 0),
        feature_at,
        jnp.where((hub_at >= 0) & (hub_at < hubs_here), hub_at + rows_here, -1),
    )
    combined = jnp.concatenate([feature_table, hub_table], axis=0)
    matrix_one = count_matrix(local_one, rows_here + hubs_here)
    sums = jnp.dot(matrix_one, combined, preferred_element_type=jnp.float32)
    sums = lax.psum_scatter(sums.astype(jnp.bfloat16), "node", scatter_dimension=0, tiled=True)
    first_mean = (sums.astype(jnp.float32) / first_counts[:, None].astype(jnp.float32)).astype(
        jnp.bfloat16
    )
    part = jnp.dot(feature_table[:front_here], first_self, preferred_element_type=jnp.float32)
    part = part + jnp.dot(first_mean, first_pooled, preferred_element_type=jnp.float32)
    hidden = jax.nn.relu(
        lax.psum_scatter(part.astype(jnp.bfloat16), "feat", scatter_dimension=1, tiled=True)
    )
    projected = jnp.dot(hidden, second_pooled, preferred_element_type=jnp.float32)
    own = jnp.dot(hidden[:targets_here], second_self, preferred_element_type=jnp.float32)
    local_two = jnp.where(all_two >= 0, all_two - me * front_here, -1)
    matrix_two = count_matrix(local_two, front_here)
    mixed = jnp.dot(
        matrix_two, projected.astype(jnp.bfloat16), preferred_element_type=jnp.float32
    ) / all_counts.astype(jnp.float32)
    here = lax.dynamic_slice_in_dim(mixed, me * targets_here, targets_here, 0)
    mixed = lax.dynamic_update_slice_in_dim(mixed, here + own, me * targets_here, 0)
    mixed = lax.psum_scatter(mixed, ("node", "feat"), scatter_dimension=0, tiled=True)
    scale = lax.rsqrt(jnp.mean(mixed * mixed, axis=1, keepdims=True) + 1e-06)
    return (mixed * scale).astype(jnp.bfloat16)


def solution(mesh):
    return jax.shard_map(
        body,
        mesh=mesh,
        in_specs=(
            P("node", "feat"),
            P("node", "feat"),
            P("feat", None),
            P("feat", None),
            P("feat", None),
            P("feat", None),
            P("node", None),
            P("node"),
            P("node", None),
            P("node"),
        ),
        out_specs=P(("node", "feat"), None),
        check_vma=False,
    )
```

profile of v0, /device:TPU:0, one launch (start us, length us, event | category | flops | bytes accessed | tf_op | source)
XLA Modules:
  0.0 341.4 jit_solution(16329909199386390386)
XLA Ops:
  6.5 0.9 fusion.27
  7.7 0.7 fusion.25
  8.8 0.7 pad_add_fusion
  9.5 32.4 %all-gather.1 = s32[8,1,5376]{2,1,0:T(1,128)S(1)} all-gather(s32[1,1,5376]{2,1,0:T(1,128)S(1)} %reshape.59), channel_id=2, replica_groups=mesh['node'=8,'feat'=4] {'node'}, dimensions={0}, use_global_device_ids=true | all-gather | bytes 193536 | tf_op jit(solution)/shard_map/all_gather | solution.py:41
  42.0 1.8 ge.24
  43.8 2.8 reshape.57
  46.6 2.8 sub.31
  49.4 2.3 and_select_fusion
  51.7 7.9 %slice_reduce_fusion.9 = (s32[3072]{0:T(1024)S(1)}, s32[3072]{0:T(1024)S(1)}, s32[3072]{0:T(1024)S(1)}, s32[3072]{0:T(1024)S(1)}, s32[3072]{0:T(1024)S(1)}, /*in...) fusion(s32[3072,10]{1,0:T(8,128)S(1)} %and_select_fusion), kind=kLoop, calls=%fused_computation.40 | loop fusion | bytes 245760 | tf_op jit(solution)/shard_map/slice | solution.py:11
  59.7 19.4 %fusion.11 = bf16[3072,512]{1,0:T(8,128)(2,1)} fusion(s32[3072]{0:T(1024)S(1)} %get-tuple-element.6, s32[3072]{0:T(1024)S(1)} %get-tuple-element.7, s32[3072]{0:T(1024)S(1)} %get-tuple-element.8, s32[3072]{0:T(1024)S(1)} %get-tuple-element.9, s32[3072]{0:T(1024)S(1)} %get-tuple-element.10, s32[3072]{0:T(1024)S(1)} %get-tuple-element.11, ...), kind=kOutput, calls=%fused_computation.22 | convolution fusion | flops 3332227072 | bytes 4321280 | tf_op jit(solution)/shard_map/dot_general | solution.py:56
  79.1 0.6 copy-done.3
  79.8 3.6 %fusion.22 = f32[384,2048]{1,0:T(8,128)} fusion(bf16[512,2048]{1,0:T(8,128)(2,1)S(1)} %copy-done, bf16[1024,512]{1,0:T(8,128)(2,1)} %param.10), kind=kOutput, calls=%fused_computation.60 | convolution fusion | flops 805306368 | bytes 5636096 | tf_op jit(solution)/shard_map/dot_general | solution.py:61
  83.4 71.1 %reduce-scatter.4.cloned.1.call-done = bf16[384,512]{1,0:T(8,128)(2,1)} async-done(((bf16[3072,512]{1,0:T(8,128)(2,1)}), bf16[384,512]{1,0:T(8,128)(2,1)}) %reduce-scatter.4.cloned.1.call-update) | async-done | bytes 393232 | tf_op jit(solution)/shard_map/reduce_scatter | solution.py:57
  154.5 4.8 %add_convert_fusion.4 = bf16[384,2048]{1,0:T(8,128)(2,1)} fusion(f32[384,2048]{1,0:T(8,128)} %fusion.22, bf16[512,2048]{1,0:T(8,128)(2,1)} %param.13, bf16[384,512]{1,0:T(8,128)(2,1)} %reduce-scatter.4.cloned.1.call-done, f32[384]{0:T(512)S(1)} %convert_element_type.103), kind=kOutput, calls=%fused_computation.23 | convolution fusion | flops 807469056 | bytes 7210496 | tf_op jit(solution)/shard_map/dot_general | solution.py:62
  159.3 0.3 reduce-scatter.8.cloned.1.call-start
  159.7 0.9 select_n.30
  160.6 2.5 slice_reduce_fusion.14
  163.1 23.5 %reduce-scatter.6.cloned.1.call-done = bf16[384,512]{1,0:T(8,128)(2,1)} async-done(((bf16[384,2048]{1,0:T(8,128)(2,1)}), bf16[384,512]{1,0:T(8,128)(2,1)}) %reduce-scatter.6.cloned.1.call-update) | async-done | bytes 393232 | tf_op jit(solution)/shard_map/reduce_scatter | solution.py:64
  186.6 1.0 broadcast_maximum_fusion
  187.7 4.7 %convolution_divide_fusion = f32[2048,256]{1,0:T(8,128)} fusion(s32[2048]{0:T(1024)S(1)} %get-tuple-element.16, s32[2048]{0:T(1024)S(1)} %get-tuple-element.17, s32[2048]{0:T(1024)S(1)} %get-tuple-element.18, s32[2048]{0:T(1024)S(1)} %get-tuple-element.19, s32[2048]{0:T(1024)S(1)} %get-tuple-element.15, bf16[512,256]{1,0:T(8,128)(2,1)S(1)} %copy-done.4, ...), kind=kOutput, calls=%fused_computation.30 | convolution fusion | flops 515932160 | bytes 2801664 | tf_op jit(solution)/shard_map/dot_general | solution.py:70
  192.4 1.9 fusion.17
  194.2 138.1 %reduce-scatter.8.cloned.1.call-done = f32[64,256]{1,0:T(8,128)} async-done(((f32[2048,256]{1,0:T(8,128)}), f32[64,256]{1,0:T(8,128)}) %reduce-scatter.8.cloned.1.call-update) | async-done | bytes 65552 | tf_op jit(solution)/shard_map/reduce_scatter | solution.py:75
  332.4 0.9 multiply_reduce_fusion
  333.3 1.5 multiply_convert_fusion
  (29 shorter events, 0.9 us)
Async XLA Ops:
  6.5 73.2 %copy-start = (bf16[512,2048]{1,0:T(8,128)(2,1)S(1)}, bf16[512,2048]{1,0:T(8,128)(2,1)}, u32[]{:S(2)}) copy-start(bf16[512,2048]{1,0:T(8,128)(2,1)} %param.12) | copy-start | bytes 6291460
  6.5 148.0 %reduce-scatter.4.cloned.1.call-start = ((), (), s32[]{:S(2)}) async-start(), calls=%async_computation.3 | async-start | bytes 3538944 | tf_op jit(solution)/shard_map/reduce_scatter | solution.py:57
  51.7 7.9 %copy-start.2 = (bf16[1024,512]{1,0:T(8,128)(2,1)S(1)}, bf16[1024,512]{1,0:T(8,128)(2,1)}, u32[]{:S(2)}) copy-start(bf16[1024,512]{1,0:T(8,128)(2,1)} %param.10) | copy-start | bytes 3145732
  51.7 7.9 %copy-start.5 = (bf16[4,512]{1,0:T(4,128)(2,1)S(1)}, bf16[4,512]{1,0:T(4,128)(2,1)}, u32[]{:S(2)}) copy-start(bf16[4,512]{1,0:T(4,128)(2,1)} %param.11) | copy-start | bytes 12292
  79.1 0.7 copy-start.3
  79.1 107.5 %reduce-scatter.6.cloned.1.call-start = ((), (), s32[]{:S(2)}) async-start(), calls=%async_computation.4 | async-start | bytes 1966080 | tf_op jit(solution)/shard_map/reduce_scatter | solution.py:64
  159.3 173.0 %reduce-scatter.8.cloned.1.call-start = ((), (), s32[]{:S(2)}) async-start(), calls=%async_computation.5 | async-start | bytes 2162688 | tf_op jit(solution)/shard_map/reduce_scatter | solution.py:75
  160.6 27.1 %copy-start.4 = (bf16[512,256]{1,0:T(8,128)(2,1)S(1)}, bf16[512,256]{1,0:T(8,128)(2,1)}, u32[]{:S(2)}) copy-start(bf16[512,256]{1,0:T(8,128)(2,1)} %param.15) | copy-start | bytes 786436
  187.6 4.7 %copy-start.1 = (bf16[512,256]{1,0:T(8,128)(2,1)S(1)}, bf16[512,256]{1,0:T(8,128)(2,1)}, u32[]{:S(2)}) copy-start(bf16[512,256]{1,0:T(8,128)(2,1)} %param.14) | copy-start | bytes 786436
Sparse Core Ops, SparseCore 0:
  79.2 75.2 reduce-scatter.3
  159.5 27.0 reduce-scatter.5
  194.4 137.9 reduce-scatter.7
where the time goes:
time: 342 us; the launch traced here: 341 us
  waiting for transfers between devices  233 us (68%)
  matrix products  34.4 us (10%)
  blocking collectives  32.4 us (9%)
  local copies, waits for them, and re-layouts  20 us (6%)
  between operations  13.3 us (4%)
  other arithmetic  8.17 us (2%)
    reduce_scatter x1, waiting for transfers between devices, body(): lax.psum_scatter(mixed, ('node', 'feat'), scatter_dimension=0, tiled=True)  138 us
    reduce_scatter x1, waiting for transfers between devices, body(): lax.psum_scatter(sums.astype(jnp.bfloat16), 'node', scatter_dimension=0,...  71.1 us
    all_gather x1, blocking collectives, body(): everyone = lax.all_gather(packed, 'node', axis=0, tiled=True)  32.4 us
    reduce_scatter x1, waiting for transfers between devices, body(): lax.psum_scatter(part.astype(jnp.bfloat16), 'feat', scatter_dimension=1,...  23.5 us
    dot_general x1, matrix products, body(): sums = jnp.dot(matrix_one, combined, preferred_element_type=jnp.float32)  19.4 us
    slice x2, local copies, waits for them, and re-layouts, count_matrix(): total = total + (local[:, k:k + 1] == columns).astype(jnp.float32)  10.4 us
  transfers between devices with their start and end apart: 3, of which 3 were waited for; matrix products, arithmetic and copies ran while one was open for 2% of the time, Pallas kernels for 0%

commit v1 on v0

--- a/solution.py
+++ b/solution.py
@@ -38,7 +38,8 @@
     packed = jnp.concatenate([lists_one.reshape(-1), lists_two.reshape(-1), second_counts]).reshape(
         1, -1
     )
-    everyone = lax.all_gather(packed, "node", axis=0, tiled=True)
+    copies = jnp.concatenate([packed] * lax.axis_size("node"), axis=0)
+    everyone = lax.all_to_all(copies, "node", 0, 0, tiled=True)
     cut_one = front_here * fan_one
     cut_two = cut_one + targets_here * fan_two
     all_one = everyone[:, :cut_one].reshape(shards * front_here, fan_one)

time: 342 us -> 323 us (0.944)
  blocking collectives: 32.4 us -> 0 us
  starting transfers between devices: 0.31 us -> 7.62 us
  waiting for transfers between devices: 233 us -> 238 us
    all_gather x1 -> x0, blocking collectives: 32.4 us -> none  [body(): everyone = lax.all_gather(packed, 'node', axis=0, tiled=True)]
    all_to_all x0 -> x1, waiting for transfers between devices: none -> 7.57 us  [body(): everyone = lax.all_to_all(copies, 'node', 0, 0, tiled=True)]
    all_to_all x0 -> x1, starting transfers between devices: none -> 7.28 us  [body(): everyone = lax.all_to_all(copies, 'node', 0, 0, tiled=True)]
  transfers between devices with their start and end apart: 3 -> 4, of which waited for: 3 -> 4; matrix products, arithmetic and copies ran while one was open for 2% -> 2% of each run, Pallas kernels for 0% -> 0%
where the time goes in v1:
time: 323 us
  waiting for transfers between devices  238 us (74%)
  matrix products  34.4 us (11%)
  local copies, waits for them, and re-layouts  20.7 us (6%)
  between operations  13.3 us (4%)
  other arithmetic  8.17 us (3%)
  starting transfers between devices  7.62 us (2%)
    reduce_scatter x1, waiting for transfers between devices, body(): lax.psum_scatter(mixed, ('node', 'feat'), scatter_dimension=0, tiled=True)  139 us
    reduce_scatter x1, waiting for transfers between devices, body(): lax.psum_scatter(sums.astype(jnp.bfloat16), 'node', scatter_dimension=0,...  68.6 us
    reduce_scatter x1, waiting for transfers between devices, body(): lax.psum_scatter(part.astype(jnp.bfloat16), 'feat', scatter_dimension=1,...  23.5 us
    dot_general x1, matrix products, body(): sums = jnp.dot(matrix_one, combined, preferred_element_type=jnp.float32)  19.4 us
    slice x2, local copies, waits for them, and re-layouts, count_matrix(): total = total + (local[:, k:k + 1] == columns).astype(jnp.float32)  10.4 us
    all_to_all x1, waiting for transfers between devices, body(): everyone = lax.all_to_all(copies, 'node', 0, 0, tiled=True)  7.57 us
    all_to_all x1, starting transfers between devices, body(): everyone = lax.all_to_all(copies, 'node', 0, 0, tiled=True)  7.28 us
  transfers between devices with their start and end apart: 4, of which 4 were waited for; matrix products, arithmetic and copies ran while one was open for 2% of the time, Pallas kernels for 0%

profile of v1, /device:TPU:0, one launch (start us, length us, event | category | flops | bytes accessed | tf_op | source)
XLA Modules:
  0.0 322.6 jit_solution(143878566394149892)
XLA Ops:
  6.5 0.9 fusion.27
  7.7 0.7 fusion.25
  8.8 0.7 pad_add_fusion
  9.5 0.8 concatenate.10
  10.2 7.3 %all-to-all-start = ((s32[8,1,5376]{2,1,0:T(1,128)}), s32[8,1,5376]{2,1,0:T(1,128)S(1)}, u32[]{:S(2)}, u32[]{:S(2)}) async-start(s32[8,1,5376]{2,1,0:T(1,128)} %concatenate.10), calls=%async_computation | async-start | bytes 344064 | tf_op jit(solution)/shard_map/all_to_all | solution.py:42
  17.6 7.6 %all-to-all-done = s32[8,1,5376]{2,1,0:T(1,128)S(1)} async-done(((s32[8,1,5376]{2,1,0:T(1,128)}), s32[8,1,5376]{2,1,0:T(1,128)S(1)}, u32[]{:S(2)}, u32[]{:S(2)}) %all-to-all-start) | async-done | bytes 172064 | tf_op jit(solution)/shard_map/all_to_all | solution.py:42
  25.2 1.8 ge.24
  27.0 2.8 reshape.61
  29.8 2.8 sub.31
  32.6 2.3 and_select_fusion
  34.9 7.9 %slice_reduce_fusion.9 = (s32[3072]{0:T(1024)S(1)}, s32[3072]{0:T(1024)S(1)}, s32[3072]{0:T(1024)S(1)}, s32[3072]{0:T(1024)S(1)}, s32[3072]{0:T(1024)S(1)}, /*in...) fusion(s32[3072,10]{1,0:T(8,128)S(1)} %and_select_fusion), kind=kLoop, calls=%fused_computation.40 | loop fusion | bytes 245760 | tf_op jit(solution)/shard_map/slice | solution.py:11
  42.9 19.4 %fusion.11 = bf16[3072,512]{1,0:T(8,128)(2,1)} fusion(s32[3072]{0:T(1024)S(1)} %get-tuple-element.6, s32[3072]{0:T(1024)S(1)} %get-tuple-element.7, s32[3072]{0:T(1024)S(1)} %get-tuple-element.8, s32[3072]{0:T(1024)S(1)} %get-tuple-element.9, s32[3072]{0:T(1024)S(1)} %get-tuple-element.10, s32[3072]{0:T(1024)S(1)} %get-tuple-element.11, ...), kind=kOutput, calls=%fused_computation.22 | convolution fusion | flops 3332227072 | bytes 4321280 | tf_op jit(solution)/shard_map/dot_general | solution.py:57
  63.0 3.6 %fusion.22 = f32[384,2048]{1,0:T(8,128)} fusion(bf16[512,2048]{1,0:T(8,128)(2,1)S(1)} %copy-done, bf16[1024,512]{1,0:T(8,128)(2,1)} %param.10), kind=kOutput, calls=%fused_computation.60 | convolution fusion | flops 805306368 | bytes 5636096 | tf_op jit(solution)/shard_map/dot_general | solution.py:62
  66.6 68.6 %reduce-scatter.4.cloned.1.call-done = bf16[384,512]{1,0:T(8,128)(2,1)} async-done(((bf16[3072,512]{1,0:T(8,128)(2,1)}), bf16[384,512]{1,0:T(8,128)(2,1)}) %reduce-scatter.4.cloned.1.call-update) | async-done | bytes 393232 | tf_op jit(solution)/shard_map/reduce_scatter | solution.py:58
  135.2 4.8 %add_convert_fusion.4 = bf16[384,2048]{1,0:T(8,128)(2,1)} fusion(f32[384,2048]{1,0:T(8,128)} %fusion.22, bf16[512,2048]{1,0:T(8,128)(2,1)} %param.13, bf16[384,512]{1,0:T(8,128)(2,1)} %reduce-scatter.4.cloned.1.call-done, f32[384]{0:T(512)S(1)} %convert_element_type.103), kind=kOutput, calls=%fused_computation.23 | convolution fusion | flops 807469056 | bytes 7210496 | tf_op jit(solution)/shard_map/dot_general | solution.py:63
  140.4 0.9 select_n.30
  141.3 2.5 slice_reduce_fusion.14
  143.8 23.5 %reduce-scatter.6.cloned.1.call-done = bf16[384,512]{1,0:T(8,128)(2,1)} async-done(((bf16[384,2048]{1,0:T(8,128)(2,1)}), bf16[384,512]{1,0:T(8,128)(2,1)}) %reduce-scatter.6.cloned.1.call-update) | async-done | bytes 393232 | tf_op jit(solution)/shard_map/reduce_scatter | solution.py:65
  167.3 1.0 broadcast_maximum_fusion
  168.3 4.7 %convolution_divide_fusion = f32[2048,256]{1,0:T(8,128)} fusion(s32[2048]{0:T(1024)S(1)} %get-tuple-element.16, s32[2048]{0:T(1024)S(1)} %get-tuple-element.17, s32[2048]{0:T(1024)S(1)} %get-tuple-element.18, s32[2048]{0:T(1024)S(1)} %get-tuple-element.19, s32[2048]{0:T(1024)S(1)} %get-tuple-element.15, bf16[512,256]{1,0:T(8,128)(2,1)S(1)} %copy-done.4, ...), kind=kOutput, calls=%fused_computation.30 | convolution fusion | flops 515932160 | bytes 2801664 | tf_op jit(solution)/shard_map/dot_general | solution.py:71
  173.0 1.9 fusion.17
  174.9 138.6 %reduce-scatter.8.cloned.1.call-done = f32[64,256]{1,0:T(8,128)} async-done(((f32[2048,256]{1,0:T(8,128)}), f32[64,256]{1,0:T(8,128)}) %reduce-scatter.8.cloned.1.call-update) | async-done | bytes 65552 | tf_op jit(solution)/shard_map/reduce_scatter | solution.py:76
  313.6 0.9 multiply_reduce_fusion
  314.5 1.5 multiply_convert_fusion
  (30 shorter events, 1.7 us)
Async XLA Ops:
  6.5 56.4 %copy-start = (bf16[512,2048]{1,0:T(8,128)(2,1)S(1)}, bf16[512,2048]{1,0:T(8,128)(2,1)}, u32[]{:S(2)}) copy-start(bf16[512,2048]{1,0:T(8,128)(2,1)} %param.12) | copy-start | bytes 6291460
  10.2 14.9 %all-to-all-start = ((s32[8,1,5376]{2,1,0:T(1,128)}), s32[8,1,5376]{2,1,0:T(1,128)S(1)}, u32[]{:S(2)}, u32[]{:S(2)}) async-start(s32[8,1,5376]{2,1,0:T(1,128)} %concatenate.10), calls=%async_computation | async-start | bytes 344064 | tf_op jit(solution)/shard_map/all_to_all | solution.py:42
  17.5 117.7 %reduce-scatter.4.cloned.1.call-start = ((), (), s32[]{:S(2)}) async-start(), calls=%async_computation.4 | async-start | bytes 3538944 | tf_op jit(solution)/shard_map/reduce_scatter | solution.py:58
  34.9 7.9 %copy-start.2 = (bf16[1024,512]{1,0:T(8,128)(2,1)S(1)}, bf16[1024,512]{1,0:T(8,128)(2,1)}, u32[]{:S(2)}) copy-start(bf16[1024,512]{1,0:T(8,128)(2,1)} %param.10) | copy-start | bytes 3145732
  34.9 7.9 %copy-start.5 = (bf16[4,512]{1,0:T(4,128)(2,1)S(1)}, bf16[4,512]{1,0:T(4,128)(2,1)}, u32[]{:S(2)}) copy-start(bf16[4,512]{1,0:T(4,128)(2,1)} %param.11) | copy-start | bytes 12292
  62.3 0.7 copy-start.3
  62.3 105.0 %reduce-scatter.6.cloned.1.call-start = ((), (), s32[]{:S(2)}) async-start(), calls=%async_computation.5 | async-start | bytes 1966080 | tf_op jit(solution)/shard_map/reduce_scatter | solution.py:65
  140.1 173.5 %reduce-scatter.8.cloned.1.call-start = ((), (), s32[]{:S(2)}) async-start(), calls=%async_computation.6 | async-start | bytes 2162688 | tf_op jit(solution)/shard_map/reduce_scatter | solution.py:76
  141.3 27.0 %copy-start.4 = (bf16[512,256]{1,0:T(8,128)(2,1)S(1)}, bf16[512,256]{1,0:T(8,128)(2,1)}, u32[]{:S(2)}) copy-start(bf16[512,256]{1,0:T(8,128)(2,1)} %param.15) | copy-start | bytes 786436
  168.3 4.7 %copy-start.1 = (bf16[512,256]{1,0:T(8,128)(2,1)S(1)}, bf16[512,256]{1,0:T(8,128)(2,1)}, u32[]{:S(2)}) copy-start(bf16[512,256]{1,0:T(8,128)(2,1)} %param.14) | copy-start | bytes 786436
Sparse Core Ops, SparseCore 0:
  62.4 72.7 reduce-scatter.3
  140.2 27.0 reduce-scatter.5
  175.1 138.4 reduce-scatter.7
